TPU v7x, 32 devices: a whole 2x2x4 slice. The times are simulated.
32 devices in a mesh: gx: 8 (over z, x), gy: 4 (over y, core).
Axes of the slice: x: 2, y: 2, z: 4, core: 2. Of those that a mesh axis runs over, the one named last changes fastest.
Arguments:
- reference_scan: bfloat16 [128, 128, 2048], P('gx', 'gy'), may hold values from -6 to 6
- ref_gradient: bfloat16 [3, 128, 128, 2048], P(None, 'gx', 'gy'), may hold values from -6 to 6
- deformed_scan: bfloat16 [128, 128, 2048], P('gx', 'gy'), may hold values from -6 to 6
- interp_weights: bfloat16 [128, 128, 2048], P('gx', 'gy'), may hold values from 0 to 1
- sample_mask: int32 [128, 128, 2048], P('gx', 'gy'), may hold values from 0 to 1, as said below
- block_list: int32 [8, 16384], P('gx', 'gy'), may hold values from -1 to 8191, as said below
- offsets: int32 [2, 128, 128, 4], P(None, 'gx', 'gy'), may hold values from -4 to 4, as said below
Outputs:
- increment: float32 [3, 128, 128, 5], P(None, 'gx', 'gy')
- cg_residual: float32 [3, 128, 128, 5], P(None, 'gx', 'gy')
Inputs may be any that keep to these rules, and one draw needn't show every extreme that they name: sample_mask is 0 in every block of 128 voxels that its device's block_list does not name. `block_list`: each device's 4096 entries are first distinct local block indices, then -1 to the end; some device names exactly 4096 blocks. `offsets`: both ends of the range occur.
All inputs are finite; a program needn't handle non-finite values.
Results may differ from a plain program's by a relative error of at most 0.0045.
Values may be sent and summed in bfloat16 or wider, within the bound.
A program may use at most 320 MiB of HBM per device.

v0:
```python
import jax
import jax.numpy as jnp
from jax import lax
from jax.sharding import PartitionSpec as P

BOUND = 4
ITERS = 3


tikhonov = 8.0


def extended(value, sides, width):
    for axis, dim in sides:
        devices, length = (lax.axis_size(axis), value.shape[dim])
        up = [(i, (i + 1) % devices) for i in range(devices - 1)]
        down = [(j, i) for i, j in up]
        last = lax.slice_in_dim(value, length - width, length, axis=dim)
        first = lax.slice_in_dim(value, 0, width, axis=dim)
        before = lax.ppermute(last, axis, up)
        after = lax.ppermute(first, axis, down)
        value = jnp.concatenate([before, value, after], axis=dim)
    return value


def from_behind(block, axis, distance):
    devices = range(lax.axis_size(axis))
    route = [(i - distance, i) for i in devices if i - distance in devices]
    return lax.ppermute(block, axis, route)


def shape_table():
    voxel = jnp.arange(512)
    coords = [
        ((voxel // 64).astype(jnp.float32) + 0.5) / 8.0,
        ((voxel // 8 % 8).astype(jnp.float32) + 0.5) / 8.0,
        ((voxel % 8).astype(jnp.float32) + 0.5) / 8.0,
    ]
    rows = []
    for node in range(8):
        bits = [node >> 2 & 1, node >> 1 & 1, node & 1]
        value = jnp.ones((512,), jnp.float32)
        for axis_pos in range(3):
            value = value * (coords[axis_pos] if bits[axis_pos] else 1.0 - coords[axis_pos])
        rows.append(value)
    return jnp.transpose(jnp.stack(rows).reshape(8, 4, 128), (1, 0, 2))


def block_terms(grad_rows, resid_rows, mask_rows, kinds, table):
    onehot = (kinds[:, None] == jnp.arange(4)[None, :]).astype(jnp.float32)
    shapes = jnp.einsum("bk,knv->bnv", onehot, table, precision=lax.Precision.HIGHEST)
    product = shapes[:, :, None, :] * grad_rows[:, None, :, :].astype(jnp.float32)
    jacobian = product.reshape(kinds.shape[0], 24, 128).astype(jnp.bfloat16)
    weighted = jacobian * mask_rows[:, None, :]
    hessian = jnp.einsum("bdv,bev->bde", weighted, jacobian, preferred_element_type=jnp.float32)
    gradient = jnp.einsum("bdv,bv->bd", weighted, resid_rows, preferred_element_type=jnp.float32)
    return (hessian, gradient)


def run_groups(grad_rows, resid_rows, mask_rows, kinds, table):
    count = kinds.shape[0]
    groups = 4
    packed = (
        grad_rows.reshape((groups, count // groups) + grad_rows.shape[1:]),
        resid_rows.reshape(groups, count // groups, 128),
        mask_rows.reshape(groups, count // groups, 128),
        kinds.reshape(groups, count // groups),
    )
    hessian, gradient = lax.map(
        lambda parts: block_terms(parts[0], parts[1], parts[2], parts[3], table), packed
    )
    return (hessian.reshape(count, 24, 24), gradient.reshape(count, 24))


def per_device(
    reference_scan, ref_gradient, deformed_scan, interp_weights, sample_mask, block_list, offsets
):
    tile_x, tile_y, column = reference_scan.shape
    elem_depth = column // 512
    padded = extended(deformed_scan, (("gx", 0), ("gy", 1)), BOUND + 1)
    margin = BOUND + 1
    span_y = padded.shape[1]
    flat_scan = padded.reshape(padded.shape[0] * span_y, elem_depth, 512)
    pos_x = jnp.arange(tile_x)[:, None, None]
    pos_y = jnp.arange(tile_y)[None, :, None]
    source = (pos_x + offsets[0] + margin) * span_y + pos_y + offsets[1] + margin
    layer = jnp.broadcast_to(jnp.arange(elem_depth)[None, None, :], source.shape)
    near = flat_scan[source, layer].astype(jnp.float32)
    far = flat_scan[source + span_y, layer].astype(jnp.float32)
    weights = interp_weights.reshape(tile_x, tile_y, elem_depth, 512).astype(jnp.float32)
    warped = weights * near + (1.0 - weights) * far
    residual_image = (
        reference_scan.reshape(tile_x, tile_y, elem_depth, 512).astype(jnp.float32) - warped
    ).astype(jnp.bfloat16)
    local_blocks = tile_x * tile_y * elem_depth * 4
    elements = local_blocks // 4
    grad_blocks = jnp.moveaxis(ref_gradient.reshape(3, local_blocks, 128), 0, 1)
    resid_blocks = residual_image.reshape(local_blocks, 128)
    mask_blocks = sample_mask.reshape(local_blocks, 128)
    entries = block_list.reshape(-1)
    listed = entries >= 0
    safe = jnp.maximum(entries, 0)
    table = shape_table()
    marks = jnp.zeros((local_blocks,), jnp.bfloat16).at[safe].add(listed.astype(jnp.bfloat16))
    mask_rows = mask_blocks.astype(jnp.bfloat16) * marks[:, None]
    hessian, gradient = run_groups(
        grad_blocks, resid_blocks, mask_rows, jnp.arange(local_blocks) % 4, table
    )
    elem_hess = hessian.reshape(elements, 4, 24, 24).sum(axis=1)
    elem_load = gradient.reshape(elements, 4, 24).sum(axis=1)
    stiffness = jnp.transpose(elem_hess, (1, 2, 0))
    loads = jnp.transpose(elem_load, (1, 0))

    def spread(field):
        upper_x = from_behind(field[:, :1], "gx", -1)
        wide = jnp.concatenate([field, upper_x], axis=1)
        upper_y = from_behind(wide[:, :, :1], "gy", -1)
        wide = jnp.concatenate([wide, upper_y], axis=2)
        pieces = []
        for node in range(8):
            i_bit, j_bit, l_bit = (node >> 2 & 1, node >> 1 & 1, node & 1)
            pieces.append(
                wide[:, i_bit : i_bit + tile_x, j_bit : j_bit + tile_y, l_bit : l_bit + elem_depth]
            )
        return jnp.stack(pieces).reshape(24, elements)

    def collect(values):
        parts = values.reshape(8, 3, tile_x, tile_y, elem_depth)
        total = jnp.zeros((3, tile_x + 1, tile_y + 1, elem_depth + 1), jnp.float32)
        for node in range(8):
            i_bit, j_bit, l_bit = (node >> 2 & 1, node >> 1 & 1, node & 1)
            total = total + jnp.pad(
                parts[node], ((0, 0), (i_bit, 1 - i_bit), (j_bit, 1 - j_bit), (l_bit, 1 - l_bit))
            )
        passed_y = from_behind(total[:, :, tile_y:], "gy", 1)
        total = total[:, :, :tile_y].at[:, :, 0:1].add(passed_y)
        passed_x = from_behind(total[:, tile_x:], "gx", 1)
        return total[:, :tile_x].at[:, 0:1].add(passed_x)

    def operate(field):
        images = jnp.einsum("nzr,zr->nr", stiffness, spread(field), precision=lax.Precision.HIGHEST)
        return collect(images) + tikhonov * field

    def two_products(vector, image):
        return lax.psum((jnp.sum(vector * vector), jnp.sum(vector * image)), ("gx", "gy"))

    rhs = collect(loads)
    increment = jnp.zeros_like(rhs)
    cg_residual = rhs
    image = operate(cg_residual)
    norm_now, product = two_products(cg_residual, image)
    step_size = norm_now / product
    direction, along = (cg_residual, image)
    for sweep in range(ITERS):
        increment = increment + step_size * direction
        cg_residual = cg_residual - step_size * along
        if sweep + 1 < ITERS:
            image = operate(cg_residual)
            norm_next, product = two_products(cg_residual, image)
            factor = norm_next / norm_now
            step_size = norm_next / (product - factor * norm_next / step_size)
            direction = cg_residual + factor * direction
            along = image + factor * along
            norm_now = norm_next
    return (increment, cg_residual)


def solution(mesh):
    return jax.shard_map(
        per_device,
        mesh=mesh,
        in_specs=(
            P("gx", "gy", None),
            P(None, "gx", "gy", None),
            P("gx", "gy", None),
            P("gx", "gy", None),
            P("gx", "gy", None),
            P("gx", "gy"),
            P(None, "gx", "gy", None),
        ),
        out_specs=(P(None, "gx", "gy", None), P(None, "gx", "gy", None)),
        check_vma=False,
    )
```

profile of v0, /device:TPU:0, one launch (start us, length us, event | category | flops | bytes accessed | tf_op | source)
XLA Modules:
  0.0 903.2 jit_solution(9337056668083446105)
XLA Ops:
  30.8 28.9 %scatter_custom_fusion = bf16[8192]{0:T(1024)(128)(2,1)S(1)} fusion(s32[4096]{0:T(1024)S(1)} %bitcast.232, bf16[4096]{0:T(1024)(128)(2,1)S(1)} %fusion.63, bf16[]{:T(256)} %constant.278.clone.1), kind=kCustom, calls=%fused_computation.157 | custom fusion | flops 4096 | bytes 16386 | tf_op jit(solution)/shard_map/scatter-add | solution.py:104
  59.7 10.5 %reshape.725 = bf16[3,8192,128]{2,1,0:T(8,128)(2,1)} reshape(bf16[3,16,32,2048]{3,2,1,0:T(8,128)(2,1)} %param.26) | data formatting | bytes 12582912 | tf_op jit(solution)/shard_map/reshape | solution.py:97
  80.8 6.1 pad_maximum_fusion
  91.7 10.6 %reshape.727 = bf16[1092,4,512]{2,1,0:T(4,128)(2,1)} reshape(bf16[26,42,2048]{2,1,0:T(8,128)(2,1)} %copy.263) | data formatting | bytes 8945664 | tf_op jit(solution)/shard_map/reshape | solution.py:83
  102.3 26.3 %gather_fusion = bf16[2048,512]{1,0:T(8,128)(2,1)S(1)} fusion(bf16[1092,4,512]{2,1,0:T(4,128)(2,1)} %reshape.727, s32[2048]{0:T(1024)S(1)} %reshape.737), kind=kCustom, calls=%fused_computation | custom fusion | bytes 4210688 | tf_op jit(solution)/shard_map/gather | solution.py:88
  131.4 26.4 %gather_fusion.1 = bf16[2048,512]{1,0:T(8,128)(2,1)S(1)} fusion(bf16[1092,4,512]{2,1,0:T(4,128)(2,1)} %reshape.727, s32[2048]{0:T(1024)S(1)} %reshape.743), kind=kCustom, calls=%fused_computation.1 | custom fusion | bytes 4210688 | tf_op jit(solution)/shard_map/gather | solution.py:89
  160.7 6.7 subtract_convert_fusion
  167.4 264.3 %while.20 = (s32[]{:T(128)}, f32[4,2048,24,24]{3,2,1,0:T(8,128)}, f32[4,2048,24]{1,2,0:T(8,128)}, s32[4,2048]{1,0:T(4,128)S(1)}, f32[4,8,128]{2,0,1:T(4,128)S(1)...) while((s32[]{:T(128)}, f32[4,2048,24,24]{3,2,1,0:T(8,128)}, ...), condition=%wide.region_2.3_spmd, body=%wide.region_1.2_spmd.sunk | while | flops 434905088 | bytes 179807376 | solution.py:69
  177.6 6.8 broadcast_multiply_fusion.3
  184.4 27.1 %bitcast_dynamic-update-slice_fusion.4 = f32[4,2048,24,24]{3,2,1,0:T(8,128)} fusion(f32[4,2048,24,24]{3,2,1,0:T(8,128)} %get-tuple-element.346, s32[]{:T(128)} %get-tuple-element.345, bf16[2048,24,128]{2,0,1:T(8,128)(2,1)} %bitcast.212, bf16[2048,24,128]{2,0,1:T(8,128)(2,1)} %broadcast_multiply_fusion.3), kind=kOutput, calls=%fused_computation.3.clone.1 | convolution fusion | flops 301989888 | bytes 50332160 | tf_op jit(solution)/shard_map/while/body/eval_jaxpr/bdv,bev->bde/dot_general | solution.py:55
  211.5 20.8 %fusion.102 = f32[2048,1,24]{2,1,0:T(1,128)S(1)} fusion(bf16[2048,24,128]{2,0,1:T(8,128)(2,1)} %broadcast_multiply_fusion.3, bf16[2048,128,1]{1,0,2:T(8,128)(2,1)S(1)} %dynamic-slice_bitcast_fusion.5), kind=kOutput, calls=%fused_computation.7.clone.1 | convolution fusion | flops 12582912 | bytes 13303808 | tf_op jit(solution)/shard_map/while/body/eval_jaxpr/bdv,bv->bd/dot_general | solution.py:56
  243.5 6.8 broadcast_multiply_fusion.3
  250.3 27.0 %bitcast_dynamic-update-slice_fusion.4 = f32[4,2048,24,24]{3,2,1,0:T(8,128)} fusion(f32[4,2048,24,24]{3,2,1,0:T(8,128)} %get-tuple-element.346, s32[]{:T(128)} %get-tuple-element.345, bf16[2048,24,128]{2,0,1:T(8,128)(2,1)} %bitcast.212, bf16[2048,24,128]{2,0,1:T(8,128)(2,1)} %broadcast_multiply_fusion.3), kind=kOutput, calls=%fused_computation.3.clone.1 | convolution fusion | flops 301989888 | bytes 50332160 | tf_op jit(solution)/shard_map/while/body/eval_jaxpr/bdv,bev->bde/dot_general | solution.py:55
  277.4 20.8 %fusion.102 = f32[2048,1,24]{2,1,0:T(1,128)S(1)} fusion(bf16[2048,24,128]{2,0,1:T(8,128)(2,1)} %broadcast_multiply_fusion.3, bf16[2048,128,1]{1,0,2:T(8,128)(2,1)S(1)} %dynamic-slice_bitcast_fusion.5), kind=kOutput, calls=%fused_computation.7.clone.1 | convolution fusion | flops 12582912 | bytes 13303808 | tf_op jit(solution)/shard_map/while/body/eval_jaxpr/bdv,bv->bd/dot_general | solution.py:56
  309.4 6.8 broadcast_multiply_fusion.3
  316.2 27.0 %bitcast_dynamic-update-slice_fusion.4 = f32[4,2048,24,24]{3,2,1,0:T(8,128)} fusion(f32[4,2048,24,24]{3,2,1,0:T(8,128)} %get-tuple-element.346, s32[]{:T(128)} %get-tuple-element.345, bf16[2048,24,128]{2,0,1:T(8,128)(2,1)} %bitcast.212, bf16[2048,24,128]{2,0,1:T(8,128)(2,1)} %broadcast_multiply_fusion.3), kind=kOutput, calls=%fused_computation.3.clone.1 | convolution fusion | flops 301989888 | bytes 50332160 | tf_op jit(solution)/shard_map/while/body/eval_jaxpr/bdv,bev->bde/dot_general | solution.py:55
  343.3 20.8 %fusion.102 = f32[2048,1,24]{2,1,0:T(1,128)S(1)} fusion(bf16[2048,24,128]{2,0,1:T(8,128)(2,1)} %broadcast_multiply_fusion.3, bf16[2048,128,1]{1,0,2:T(8,128)(2,1)S(1)} %dynamic-slice_bitcast_fusion.5), kind=kOutput, calls=%fused_computation.7.clone.1 | convolution fusion | flops 12582912 | bytes 13303808 | tf_op jit(solution)/shard_map/while/body/eval_jaxpr/bdv,bv->bd/dot_general | solution.py:56
  375.3 6.8 broadcast_multiply_fusion.3
  382.1 27.1 %bitcast_dynamic-update-slice_fusion.4 = f32[4,2048,24,24]{3,2,1,0:T(8,128)} fusion(f32[4,2048,24,24]{3,2,1,0:T(8,128)} %get-tuple-element.346, s32[]{:T(128)} %get-tuple-element.345, bf16[2048,24,128]{2,0,1:T(8,128)(2,1)} %bitcast.212, bf16[2048,24,128]{2,0,1:T(8,128)(2,1)} %broadcast_multiply_fusion.3), kind=kOutput, calls=%fused_computation.3.clone.1 | convolution fusion | flops 301989888 | bytes 50332160 | tf_op jit(solution)/shard_map/while/body/eval_jaxpr/bdv,bev->bde/dot_general | solution.py:55
  409.2 20.8 %fusion.102 = f32[2048,1,24]{2,1,0:T(1,128)S(1)} fusion(bf16[2048,24,128]{2,0,1:T(8,128)(2,1)} %broadcast_multiply_fusion.3, bf16[2048,128,1]{1,0,2:T(8,128)(2,1)S(1)} %dynamic-slice_bitcast_fusion.5), kind=kOutput, calls=%fused_computation.7.clone.1 | convolution fusion | flops 12582912 | bytes 13303808 | tf_op jit(solution)/shard_map/while/body/eval_jaxpr/bdv,bv->bd/dot_general | solution.py:56
  435.3 10.4 %reduce_sum.72 = f32[2048,24]{1,0:T(8,128)S(1)} reduce(f32[2048,4,24]{2,1,0:T(4,128)} %bitcast.215, f32[]{:T(128)} %constant.271.clone.1), dimensions={1}, to_apply=%region_3.4 | reduce | flops 147456 | bytes 983044 | tf_op jit(solution)/shard_map/reduce_sum | solution.py:110
  492.9 10.0 %collective-permute-start.4 = (f32[3,17,1,5]{3,2,1,0:T(1,128)S(1)}, f32[3,17,1,5]{3,2,1,0:T(1,128)S(1)}, u32[]{:S(2)}, u32[]{:S(2)}) collective-permute-start(f32[3,17,1,5]{3,2,1,0:T(1,128)S(1)} %slice.627), channel_id=1, source_target_pairs={{0,1},{1,2},{2,3},{4,5},{5,6},{6,7},{8,9},{9,10},{10,11},{12,13},{... | collective-permute-start | bytes 3068 | tf_op jit(solution)/shard_map/ppermute | solution.py:29
  508.7 41.1 %reduce_sum.74 = f32[2048,24,24]{2,1,0:T(8,128)} reduce(f32[2048,4,24,24]{3,2,1,0:T(8,128)} %bitcast.40, f32[]{:T(128)} %constant.271.clone.1), dimensions={1}, to_apply=%region_6.7 | reduce | flops 3538944 | bytes 23592964 | tf_op jit(solution)/shard_map/reduce_sum | solution.py:109
  565.6 6.7 reshape.728
  572.6 14.2 %fusion.14 = f32[2048,24]{1,0:T(8,128)S(1)} fusion(f32[2048,24,24]{2,1,0:T(8,128)} %reduce_sum.74, f32[2048,24]{1,0:T(8,128)S(1)} %copy.307), kind=kLoop, calls=%fused_computation.24 | loop fusion | flops 2310144 | bytes 5111808
  614.2 42.2 %all-reduce.34 = (f32[]{:T(128)}, f32[]{:T(128)}) all-reduce(f32[]{:T(128)} %get-tuple-element.220, f32[]{:T(128)} %get-tuple-element.219), channel_id=1, replica_groups=mesh['gx'=8,'gy'=4] {'gx','gy'}, use_global_device_ids=true, to_apply=%region_5.6 | all-reduce | flops 2 | bytes 16 | tf_op jit(solution)/shard_map/psum | solution.py:145
  673.8 6.7 reshape.729
  681.8 15.3 %fusion.15 = f32[2048,24]{1,0:T(8,128)} fusion(f32[2048,24,24]{2,1,0:T(8,128)} %reduce_sum.74, f32[2048,24]{1,0:T(8,128)} %copy.308), kind=kLoop, calls=%fused_computation.25 | loop fusion | flops 2310144 | bytes 5111808
  729.8 42.7 %all-reduce.33 = (f32[]{:T(128)}, f32[]{:T(128)}) all-reduce(f32[]{:T(128)} %get-tuple-element.218, f32[]{:T(128)} %get-tuple-element.217), channel_id=1, replica_groups=mesh['gx'=8,'gy'=4] {'gx','gy'}, use_global_device_ids=true, to_apply=%region_10.11 | all-reduce | flops 2 | bytes 16 | tf_op jit(solution)/shard_map/psum | solution.py:145
  795.3 7.2 reshape.730
  803.8 15.2 %fusion.16 = f32[2048,24]{1,0:T(8,128)} fusion(f32[2048,24,24]{2,1,0:T(8,128)} %reduce_sum.74, f32[2048,24]{1,0:T(8,128)S(1)} %copy.309), kind=kLoop, calls=%fused_computation.26 | loop fusion | flops 2310144 | bytes 5111808
  850.0 42.0 %all-reduce.32 = (f32[]{:T(128)}, f32[]{:T(128)}) all-reduce(f32[]{:T(128)} %get-tuple-element.216, f32[]{:T(128)} %get-tuple-element.215), channel_id=1, replica_groups=mesh['gx'=8,'gy'=4] {'gx','gy'}, use_global_device_ids=true, to_apply=%region_14.15 | all-reduce | flops 2 | bytes 16 | tf_op jit(solution)/shard_map/psum | solution.py:145
  (234 shorter events, 303.5 us)
Async XLA Ops:
  0.6 12.1 %copy-start.6 = (s32[1,4096]{1,0:T(1,128)S(1)}, s32[1,4096]{1,0:T(1,128)}, u32[]{:S(2)}) copy-start(s32[1,4096]{1,0:T(1,128)} %param.30) | copy-start | bytes 49156
  0.6 12.2 %copy-start.5 = (s32[2,16,32,4]{2,3,1,0:T(4,128)S(1)}, s32[2,16,32,4]{2,3,1,0:T(4,128)}, u32[]{:S(2)}) copy-start(s32[2,16,32,4]{2,3,1,0:T(4,128)} %param.31) | copy-start | bytes 49156
  3.0 67.5 %collective-permute-start = (bf16[5,32,2048]{2,1,0:T(8,128)(2,1)}, bf16[5,32,2048]{2,1,0:T(8,128)(2,1)}, u32[]{:S(2)}, u32[]{:S(2)}) collective-permute-start(bf16[5,32,2048]{2,1,0:T(8,128)(2,1)} %get-tuple-element.249), channel_id=1, source_target_pairs={{0,4},{4,8},{8,12},{12,16},{16,20},{20,24},{24,28},{1,5},{5,9},{9,... | collective-permute-start | bytes 1966088 | tf_op jit(solution)/shard_map/ppermute | solution.py:20
  8.7 63.3 %collective-permute-start.1 = (bf16[5,32,2048]{2,1,0:T(8,128)(2,1)S(1)}, bf16[5,32,2048]{2,1,0:T(8,128)(2,1)}, u32[]{:S(2)}, u32[]{:S(2)}) collective-permute-start(bf16[5,32,2048]{2,1,0:T(8,128)(2,1)S(1)} %get-tuple-element.250), channel_id=1, source_target_pairs={{4,0},{8,4},{12,8},{16,12},{20,16},{24,20},{28,24},{5,1},{9,5},{13... | collective-permute-start | bytes 1966088 | tf_op jit(solution)/shard_map/ppermute | solution.py:21
  70.3 6.6 copy-start.1
  74.0 5.1 collective-permute-start.2
  75.4 5.4 collective-permute-start.3
  176.1 8.3 copy-start
  242.0 8.3 copy-start
  307.9 8.3 copy-start
  373.8 8.3 copy-start
  450.3 27.7 %copy-start.3 = (f32[3,2048]{0,1:T(8,128)S(1)}, f32[3,2048]{0,1:T(8,128)}, u32[]{:S(2)}) copy-start(f32[3,2048]{0,1:T(8,128)} %get-tuple-element.254) | copy-start | bytes 73732
  492.9 10.8 %collective-permute-start.4 = (f32[3,17,1,5]{3,2,1,0:T(1,128)S(1)}, f32[3,17,1,5]{3,2,1,0:T(1,128)S(1)}, u32[]{:S(2)}, u32[]{:S(2)}) collective-permute-start(f32[3,17,1,5]{3,2,1,0:T(1,128)S(1)} %slice.627), channel_id=1, source_target_pairs={{0,1},{1,2},{2,3},{4,5},{5,6},{6,7},{8,9},{9,10},{10,11},{12,13},{... | collective-permute-start | bytes 3068 | tf_op jit(solution)/shard_map/ppermute | solution.py:29
  504.0 46.0 %collective-permute-start.5 = (f32[3,1,32,5]{3,2,1,0:T(8,128)S(1)}, f32[3,1,32,5]{3,2,1,0:T(8,128)S(1)}, u32[]{:S(2)}, u32[]{:S(2)}) collective-permute-start(f32[3,1,32,5]{3,2,1,0:T(8,128)S(1)} %slice.630), channel_id=1, source_target_pairs={{0,4},{4,8},{8,12},{12,16},{16,20},{20,24},{24,28},{1,5},{5,9},{9,... | collective-permute-start | bytes 5768 | tf_op jit(solution)/shard_map/ppermute | solution.py:29
  549.9 6.0 collective-permute-start.6
  556.0 3.1 collective-permute-start.7
  601.3 5.5 collective-permute-start.8
  607.0 6.3 collective-permute-start.9
  657.9 6.2 collective-permute-start.10
  664.2 3.1 collective-permute-start.11
  715.1 5.6 collective-permute-start.12
  723.2 4.9 collective-permute-start.13
  728.9 47.4 %copy-start.2 = (f32[3,16,32,5]{3,2,1,0:T(8,128)}, f32[3,16,32,5]{3,2,1,0:T(8,128)S(1)}, u32[]{:S(2)}) copy-start(f32[3,16,32,5]{3,2,1,0:T(8,128)S(1)} %fusion.51) | copy-start | bytes 92164
  779.4 6.2 collective-permute-start.14
  785.7 3.1 collective-permute-start.15
  837.0 5.5 collective-permute-start.16
  842.7 0.9 copy-start.4
  843.6 4.7 collective-permute-start.17
where the time goes:
time: 914 us; the launch traced here: 903 us
  local copies, waits for them, and re-layouts  260 us (28%)
  other arithmetic  222 us (24%)
  matrix products  205 us (22%)
  blocking collectives  127 us (14%)
  starting transfers between devices  57 us (6%)
  waiting for transfers between devices  20.1 us (2%)
  between operations  11.3 us (1%)
    psum x3, blocking collectives, two_products(): lax.psum((jnp.sum(vector * vector), jnp.sum(vector * image)), ('gx', 'gy'))  127 us
    dot_general x4, matrix products, block_terms(): jnp.einsum('bdv,bev->bde', weighted, jacobian, preferred_element_type=jnp...  108 us
    dot_general x4, matrix products, block_terms(): jnp.einsum('bdv,bv->bd', weighted, resid_rows, preferred_element_type=jnp...  83.3 us
    squeeze x32, local copies, waits for them, and re-layouts, collect(): parts[node]  75.9 us
    unnamed x16, other arithmetic  51.3 us
    ppermute x14, starting transfers between devices, from_behind(): return lax.ppermute(block, axis, route)  47.2 us
    reduce_sum x1, other arithmetic, per_device(): elem_hess = hessian.reshape(elements, 4, 24, 24).sum(axis=1)  41.1 us
    scatter-add x1, other arithmetic, per_device(): jnp.zeros((local_blocks,), jnp.bfloat16).at[safe]  28.9 us
  transfers between devices with their start and end apart: 18, of which 13 were waited for; matrix products, arithmetic and copies ran while one was open for 13% of the time, Pallas kernels for 0%

commit v1 on v0

v1 whole, which is shorter than its diff:
```python
import functools

import jax
import jax.numpy as jnp
from jax import lax
from jax.experimental import pallas as pl
from jax.experimental.pallas import tpu as pltpu
from jax.sharding import PartitionSpec as P

BOUND = 4
ITERS = 3

tikhonov = 8.0

NODES = [(n >> 2 & 1, n >> 1 & 1, n & 1) for n in range(8)]
PAIRS = [(c, d) for c in range(3) for d in range(c, 3)]
PAIR_OF = {(c, d): PAIRS.index((min(c, d), max(c, d))) for c in range(3) for d in range(3)}
MESH = pl.DeviceIdType.MESH


def extended(value, axis, dim, before_width, after_width):
    devices, length = (lax.axis_size(axis), value.shape[dim])
    up = [(i, i + 1) for i in range(devices - 1)]
    down = [(j, i) for i, j in up]
    last = lax.slice_in_dim(value, length - before_width, length, axis=dim)
    first = lax.slice_in_dim(value, 0, after_width, axis=dim)
    before = lax.ppermute(last, axis, up)
    after = lax.ppermute(first, axis, down)
    return jnp.concatenate([before, value, after], axis=dim)


def split3(table):
    first = table.astype(jnp.bfloat16)
    rest = table - first.astype(jnp.float32)
    second = rest.astype(jnp.bfloat16)
    third = (rest - second.astype(jnp.float32)).astype(jnp.bfloat16)
    return [first, second, third]


def tables():
    voxel = jnp.arange(512)
    coords = [
        ((voxel // 64).astype(jnp.float32) + 0.5) / 8.0,
        ((voxel // 8 % 8).astype(jnp.float32) + 0.5) / 8.0,
        ((voxel % 8).astype(jnp.float32) + 0.5) / 8.0,
    ]
    linear = [[1.0 - t, t] for t in coords]
    quad = [[s[0] * s[0], s[0] * s[1], s[1] * s[1]] for s in linear]
    shapes = jnp.stack([linear[0][i] * linear[1][j] * linear[2][l] for i, j, l in NODES])
    squares = jnp.stack(
        [quad[0][a] * quad[1][b] * quad[2][c] for a in range(3) for b in range(3) for c in range(3)]
    )
    squares = jnp.pad(squares, ((0, 5), (0, 0)))
    square_table = jnp.concatenate(split3(squares), axis=0)
    shape_table = jnp.concatenate(split3(shapes) + [jnp.zeros((8, 512), jnp.bfloat16)], axis=0)
    return (square_table, shape_table)


def put_split(value, high_ref, low_ref, rows, lanes):
    high = value.astype(jnp.bfloat16)
    high_ref[rows, lanes] = high
    low_ref[rows, lanes] = (value - high.astype(jnp.float32)).astype(jnp.bfloat16)


def contract(table, part):
    return lax.dot_general(
        table, part, (((1,), (1,)), ((), ())), preferred_element_type=jnp.float32
    )


def hessian_kernel(depth, table_ref, grad_ref, mask_ref, out_ref, high_ref, low_ref):
    step = pl.program_id(0)
    tile_y = mask_ref.shape[1]
    wide = depth * tile_y
    for layer in range(depth):
        for chunk in range(4):
            source = pl.ds(layer * 512 + chunk * 128, 128)
            lanes = pl.ds(chunk * 128, 128)
            mask = mask_ref[0, :, source].astype(jnp.float32)
            grads = [grad_ref[c, 0, :, source].astype(jnp.float32) for c in range(3)]
            masked = [mask * g for g in grads]
            for q, (c, d) in enumerate(PAIRS):
                rows = pl.ds(q * wide + layer * tile_y, tile_y)
                put_split(masked[c] * grads[d], high_ref, low_ref, rows, lanes)
    table = table_ref[...]
    for q in range(6):
        rows = pl.ds(q * wide, wide)
        total = contract(table, high_ref[rows, :]) + contract(table, low_ref[rows, :])
        value = total[0:32] + total[32:64] + total[64:96]
        out_ref[q, :, pl.ds(step, 1), :] = value[:, None, :]


def load_kernel(
    depth,
    span_y,
    source_ref,
    table_ref,
    padded_ref,
    scan_ref,
    weight_ref,
    grad_ref,
    mask_ref,
    out_ref,
    wide_ref,
    near_ref,
    far_ref,
    high_ref,
    low_ref,
):
    step = pl.program_id(0)
    tile_y = mask_ref.shape[1]
    wide = depth * tile_y

    @pl.when(step == 0)
    def _():
        def convert(i, carry):
            wide_ref[pl.ds(pl.multiple_of(i * span_y, 8), span_y), :] = padded_ref[i].astype(
                jnp.float32
            )
            return carry

        lax.fori_loop(0, padded_ref.shape[0], convert, 0)

    def fetch(block, carry):
        for inner in range(4):
            y = block * 4 + inner
            for layer in range(depth):
                row = source_ref[(step * tile_y + y) * depth + layer]
                lanes = pl.ds(layer * 512, 512)
                near_ref[pl.ds(y, 1), lanes] = wide_ref[pl.ds(row, 1), lanes]
                far_ref[pl.ds(y, 1), lanes] = wide_ref[pl.ds(row + span_y, 1), lanes]
        return carry

    lax.fori_loop(0, tile_y // 4, fetch, 0)
    for layer in range(depth):
        for chunk in range(4):
            source = pl.ds(layer * 512 + chunk * 128, 128)
            lanes = pl.ds(chunk * 128, 128)
            weight = weight_ref[0, :, source].astype(jnp.float32)
            warped = weight * near_ref[:, source] + (1.0 - weight) * far_ref[:, source]
            image = scan_ref[0, :, source].astype(jnp.float32) - warped
            image = image.astype(jnp.bfloat16).astype(jnp.float32)
            image = image * mask_ref[0, :, source].astype(jnp.float32)
            for c in range(3):
                rows = pl.ds(c * wide + layer * tile_y, tile_y)
                value = image * grad_ref[c, 0, :, source].astype(jnp.float32)
                put_split(value, high_ref, low_ref, rows, lanes)
    table = table_ref[...]
    for c in range(3):
        rows = pl.ds(c * wide, wide)
        total = contract(table, high_ref[rows, :]) + contract(table, low_ref[rows, :])
        value = total[0:8] + total[8:16] + total[16:24]
        out_ref[c, :, pl.ds(step, 1), :] = value[:, None, :]


def solve_kernel(
    sizes,
    tile_y,
    hess_ref,
    load_ref,
    inc_ref,
    res_ref,
    field_ref,
    image_ref,
    out_x,
    out_y,
    out_c,
    in_x,
    in_y,
    in_c,
    own_x,
    got_x,
    own_y,
    got_y,
    send_sems,
    recv_sems,
    send_x,
    recv_x,
    send_y,
    recv_y,
):
    n_gx, n_gy = sizes
    tile_x, width = (hess_ref.shape[2], hess_ref.shape[3])
    gx = lax.axis_index("gx")
    gy = lax.axis_index("gy")
    in_x[...] = jnp.zeros_like(in_x)
    in_y[...] = jnp.zeros_like(in_y)
    in_c[...] = jnp.zeros_like(in_c)

    barrier = pltpu.get_barrier_semaphore()
    for k in range(1, n_gx):
        pl.semaphore_signal(barrier, inc=1, device_id=((gx + k) % n_gx, gy), device_id_type=MESH)
    for k in range(1, n_gy):
        pl.semaphore_signal(barrier, inc=1, device_id=(gx, (gy + k) % n_gy), device_id_type=MESH)
    low = jnp.logical_and(gx > 0, gy > 0)
    high = jnp.logical_and(gx < n_gx - 1, gy < n_gy - 1)

    @pl.when(low)
    def _():
        pl.semaphore_signal(barrier, inc=1, device_id=(gx - 1, gy - 1), device_id_type=MESH)

    @pl.when(high)
    def _():
        pl.semaphore_signal(barrier, inc=1, device_id=(gx + 1, gy + 1), device_id_type=MESH)

    corners = jnp.where(low, 1, 0) + jnp.where(high, 1, 0)
    pl.semaphore_wait(barrier, n_gx - 1 + n_gy - 1 + corners)

    lane = lax.broadcasted_iota(jnp.int32, (1, tile_x, width), 2)
    row = lax.broadcasted_iota(jnp.int32, (1, tile_x, width), 1)
    in_tile = lane % tile_y
    first_y = in_tile == 0
    last_y = in_tile == tile_y - 1
    first_x = row == 0
    last_x = row == tile_x - 1
    topmost = lane >= width - tile_y
    above = lane >= tile_y

    def copies(phase, dx, dy):
        def make(k, src, dst, target):
            return pltpu.make_async_remote_copy(
                src_ref=src.at[phase],
                dst_ref=dst.at[phase],
                send_sem=send_sems.at[phase, k],
                recv_sem=recv_sems.at[phase, k],
                device_id=target,
                device_id_type=MESH,
            )

        up = dx > 0
        send_gx, recv_gx = (gx < n_gx - 1, gx > 0) if up else (gx > 0, gx < n_gx - 1)
        send_gy, recv_gy = (gy < n_gy - 1, gy > 0) if up else (gy > 0, gy < n_gy - 1)
        return [
            (make(0, out_x, in_x, (gx + dx, gy)), send_gx, recv_gx),
            (make(1, out_y, in_y, (gx, gy + dy)), send_gy, recv_gy),
            (
                make(2, out_c, in_c, (gx + dx, gy + dy)),
                jnp.logical_and(send_gx, send_gy),
                jnp.logical_and(recv_gx, recv_gy),
            ),
        ]

    def start(phase, step):
        for copy, sends, _ in copies(phase, step, step):
            pl.when(sends)(copy.start)

    def arrive(phase, step):
        for copy, _, receives in copies(phase, step, step):
            pl.when(receives)(copy.wait_recv)

    def finish(phase, step):
        for copy, sends, _ in copies(phase, step, step):
            pl.when(sends)(copy.wait_send)

    def roll(value, shift, axis):
        return pltpu.roll(value, shift % value.shape[axis], axis)

    def shift_x(value):
        return jnp.where(first_x, 0.0, roll(value, 1, 1))

    def collect(phase):
        folded = {}
        for i in range(2):
            for j in range(2):
                under = image_ref[pl.ds((4 * i + 2 * j) * 3, 3)]
                over = image_ref[pl.ds((4 * i + 2 * j + 1) * 3, 3)]
                main = under + jnp.where(above, roll(over, tile_y, 2), 0.0)
                top = jnp.where(topmost, over, 0.0)
                folded[i, j] = jnp.concatenate([main, top], axis=0)
        kept, passed = ([], [])
        for i in range(2):
            kept.append(folded[i, 0] + jnp.where(first_y, 0.0, roll(folded[i, 1], 1, 2)))
            passed.append(jnp.where(first_y, roll(folded[i, 1], 1 - tile_y, 2), 0.0))
        out_x[phase] = kept[1][:, tile_x - 8 :, :]
        out_y[phase] = passed[0] + shift_x(passed[1])
        out_c[phase] = passed[1][:, tile_x - 8 :, :]
        start(phase, 1)
        total = kept[0] + shift_x(kept[1])
        arrive(phase, 1)
        edge = in_x[phase][:, 7:8, :] + in_c[phase][:, 7:8, :]
        return total + in_y[phase] + jnp.where(first_x, edge, 0.0)

    def spread(phase, field):
        turned = roll(field, tile_y - 1, 2)
        out_x[phase] = field[:, 0:8, :]
        out_y[phase] = turned
        out_c[phase] = turned[:, 0:8, :]
        start(phase, -1)
        next_x = roll(field, -1, 1)
        next_y = roll(field, -1, 2)

        def place(i, j, value):
            main, top = (value[0:3], value[3:6])
            field_ref[pl.ds((4 * i + 2 * j) * 3, 3)] = main
            field_ref[pl.ds((4 * i + 2 * j + 1) * 3, 3)] = jnp.where(
                topmost, top, roll(main, -tile_y, 2)
            )

        place(0, 0, field)
        arrive(phase, -1)
        side = in_x[phase]
        next_x = jnp.where(last_x, side[:, 0:1, :], next_x)
        next_y = jnp.where(last_y, in_y[phase], next_y)
        corner = jnp.where(last_y[:, 0:8], in_c[phase], roll(side, -1, 2))
        both = jnp.where(last_x, corner[:, 0:1, :], roll(next_y, -1, 1))
        place(1, 0, next_x)
        place(0, 1, next_y)
        place(1, 1, both)

    def apply():
        for n, (i, j, l) in enumerate(NODES):
            for c in range(3):
                total = None
                for m, (p, q, r) in enumerate(NODES):
                    kind = (i + p) * 9 + (j + q) * 3 + l + r
                    for d in range(3):
                        term = hess_ref[PAIR_OF[c, d], kind] * field_ref[3 * m + d]
                        total = term if total is None else total + term
                image_ref[3 * n + c] = total

    def reduce_over(own, got, sends, receives, slot, index, count, target):
        def make(k):
            return pltpu.make_async_remote_copy(
                src_ref=own.at[slot],
                dst_ref=got.at[slot, k - 1],
                send_sem=sends.at[slot, k - 1],
                recv_sem=receives.at[slot, k - 1],
                device_id=target((index + k) % count),
                device_id_type=MESH,
            )

        handles = [make(k) for k in range(1, count)]
        for copy in handles:
            copy.start()
        total = own[slot]
        for copy in handles:
            copy.wait_recv()
        for copy in handles:
            copy.wait_send()
        return total, [got[slot, k - 1] for k in range(1, count)]

    def in_order(index, count, mine, others):
        total = jnp.zeros_like(mine)
        for source in range(count):
            value = jnp.where(index == source, mine, 0.0)
            for k in range(1, count):
                value = jnp.where((index - k + count) % count == source, others[k - 1], value)
            total = total + value
        return total

    def two_products(slot, vector, image):
        one = jnp.sum(jnp.sum(vector * vector, axis=0), axis=0, keepdims=True)
        two = jnp.sum(jnp.sum(vector * image, axis=0), axis=0, keepdims=True)
        line = lax.broadcasted_iota(jnp.int32, (8, width), 0)
        own_x[slot] = jnp.where(line == 0, one, jnp.where(line == 1, two, 0.0))
        mine, others = reduce_over(
            own_x, got_x, send_x, recv_x, slot, gx, n_gx, lambda t: (t, gy)
        )
        own_y[slot] = in_order(gx, n_gx, mine, others)
        mine, others = reduce_over(
            own_y, got_y, send_y, recv_y, slot, gy, n_gy, lambda t: (gx, t)
        )
        total = in_order(gy, n_gy, mine, others)
        return (
            jnp.sum(total[0:1], axis=1, keepdims=True)[None],
            jnp.sum(total[1:2], axis=1, keepdims=True)[None],
        )

    def operate(phase, field):
        spread(phase, field)
        apply()
        return collect(phase + 1) + tikhonov * field

    for c in range(3):
        for n in range(8):
            image_ref[3 * n + c] = load_ref[c, n]
    rhs = collect(0)
    increment = jnp.zeros_like(rhs)
    residual = rhs
    image = operate(1, residual)
    norm_now, product = two_products(0, residual, image)
    step_size = norm_now / product
    direction, along = (residual, image)
    for sweep in range(ITERS):
        increment = increment + step_size * direction
        residual = residual - step_size * along
        if sweep + 1 < ITERS:
            image = operate(2 * sweep + 3, residual)
            norm_next, product = two_products(sweep + 1, residual, image)
            factor = norm_next / norm_now
            step_size = norm_next / (product - factor * norm_next / step_size)
            direction = residual + factor * direction
            along = image + factor * along
            norm_now = norm_next
    inc_ref[...] = increment
    res_ref[...] = residual
    finish(0, 1)
    for sweep in range(ITERS):
        finish(2 * sweep + 1, -1)
        finish(2 * sweep + 2, 1)


def per_device(
    reference_scan, ref_gradient, deformed_scan, interp_weights, sample_mask, block_list, offsets
):
    tile_x, tile_y, column = reference_scan.shape
    depth = column // 512
    width = depth * tile_y
    square_table, shape_table = tables()

    padded = extended(deformed_scan, "gx", 0, BOUND, BOUND + 1)
    padded = extended(padded, "gy", 1, BOUND, BOUND)
    span_x, span_y = padded.shape[:2]
    pos_x = jnp.arange(tile_x)[:, None, None]
    pos_y = jnp.arange(tile_y)[None, :, None]
    source = (pos_x + offsets[0] + BOUND) * span_y + pos_y + offsets[1] + BOUND

    voxels = pl.BlockSpec((1, tile_y, column), lambda x: (x, 0, 0))
    gradients = pl.BlockSpec((3, 1, tile_y, column), lambda x: (0, x, 0, 0))
    vmem = pl.BlockSpec(memory_space=pltpu.VMEM)
    size = tile_x * tile_y * column
    hessian = pl.pallas_call(
        functools.partial(hessian_kernel, depth),
        grid=(tile_x,),
        out_shape=jax.ShapeDtypeStruct((6, 32, tile_x, width), jnp.float32),
        in_specs=[pl.BlockSpec((96, 512), lambda x: (0, 0)), gradients, voxels],
        out_specs=pl.BlockSpec((6, 32, tile_x, width), lambda x: (0, 0, 0, 0)),
        scratch_shapes=[pltpu.VMEM((6 * width, 512), jnp.bfloat16)] * 2,
        cost_estimate=pl.CostEstimate(
            flops=size * 6 * 2 * 256, bytes_accessed=size * 10, transcendentals=0
        ),
        name="hessian",
    )(square_table, ref_gradient, sample_mask)
    load = pl.pallas_call(
        functools.partial(load_kernel, depth, span_y),
        grid=(tile_x,),
        out_shape=jax.ShapeDtypeStruct((3, 8, tile_x, width), jnp.float32),
        in_specs=[
            pl.BlockSpec(memory_space=pltpu.SMEM),
            pl.BlockSpec((32, 512), lambda x: (0, 0)),
            pl.BlockSpec((span_x, span_y, column), lambda x: (0, 0, 0)),
            voxels,
            voxels,
            gradients,
            voxels,
        ],
        out_specs=pl.BlockSpec((3, 8, tile_x, width), lambda x: (0, 0, 0, 0)),
        scratch_shapes=[
            pltpu.VMEM((span_x * span_y, column), jnp.float32),
            pltpu.VMEM((tile_y, column), jnp.float32),
            pltpu.VMEM((tile_y, column), jnp.float32),
            pltpu.VMEM((3 * width, 512), jnp.bfloat16),
            pltpu.VMEM((3 * width, 512), jnp.bfloat16),
        ],
        name="load",
    )(
        source.reshape(-1),
        shape_table,
        padded,
        reference_scan,
        interp_weights,
        ref_gradient,
        sample_mask,
    )
    n_gx, n_gy = (lax.axis_size("gx"), lax.axis_size("gy"))
    phases = 2 * ITERS + 1
    part = jax.ShapeDtypeStruct((6, tile_x, width), jnp.float32)
    dma = pltpu.SemaphoreType.DMA
    increment, residual = pl.pallas_call(
        functools.partial(solve_kernel, (n_gx, n_gy), tile_y),
        out_shape=(part, part),
        in_specs=[vmem, vmem],
        out_specs=(vmem, vmem),
        scratch_shapes=[
            pltpu.VMEM((24, tile_x, width), jnp.float32),
            pltpu.VMEM((24, tile_x, width), jnp.float32),
        ]
        + [
            pltpu.VMEM((phases, 6, rows, width), jnp.float32)
            for rows in (8, tile_x, 8, 8, tile_x, 8)
        ]
        + [
            pltpu.VMEM((ITERS, 8, width), jnp.float32),
            pltpu.VMEM((ITERS, n_gx - 1, 8, width), jnp.float32),
            pltpu.VMEM((ITERS, 8, width), jnp.float32),
            pltpu.VMEM((ITERS, n_gy - 1, 8, width), jnp.float32),
            dma((phases, 3)),
            dma((phases, 3)),
            dma((ITERS, n_gx - 1)),
            dma((ITERS, n_gx - 1)),
            dma((ITERS, n_gy - 1)),
            dma((ITERS, n_gy - 1)),
        ],
        compiler_params=pltpu.CompilerParams(collective_id=0, has_side_effects=True),
        name="solve",
    )(hessian, load)

    def nodal(value):
        main = jnp.transpose(value[:3].reshape(3, tile_x, depth, tile_y), (0, 1, 3, 2))
        return jnp.concatenate([main, value[3:, :, width - tile_y :, None]], axis=3)

    return (nodal(increment), nodal(residual))


def solution(mesh):
    return jax.shard_map(
        per_device,
        mesh=mesh,
        in_specs=(
            P("gx", "gy", None),
            P(None, "gx", "gy", None),
            P("gx", "gy", None),
            P("gx", "gy", None),
            P("gx", "gy", None),
            P("gx", "gy"),
            P(None, "gx", "gy", None),
        ),
        out_specs=(P(None, "gx", "gy", None), P(None, "gx", "gy", None)),
        check_vma=False,
    )
```

time: 914 us -> 148 us (0.16); the launches traced: 903 us -> 147 us
  local copies, waits for them, and re-layouts: 260 us -> 13.8 us
  other arithmetic: 222 us -> 8.22 us
  matrix products: 205 us -> 0 us
  blocking collectives: 127 us -> 0 us
  Pallas kernels: 0 us -> 97 us
  starting transfers between devices: 57 us -> 10.3 us
  between operations: 11.3 us -> 0.85 us
    dot_general x12 -> x0, matrix products: 205 us -> none  [the longest x4 108 us: block_terms(): jnp.einsum('bdv,bev->bde', weighted, jacobian, preferred_element_type=jnp...]
    psum x3 -> x0, blocking collectives: 127 us -> none  [two_products(): lax.psum((jnp.sum(vector * vector), jnp.sum(vector * image)), ('gx', 'gy'))]
    pallas_call x0 -> x3, Pallas kernels: none -> 97 us  [the longest x1 55.8 us: per_device(): pl.pallas_call(functools.partial(solve_kernel, (n_gx, n_gy), tile_y), out...]
    squeeze x36 -> x2, local copies, waits for them, and re-layouts: 76 us -> 0.33 us  [per_device(): source = (pos_x + offsets[0] + BOUND) * span_y + pos_y + offsets[1] + BOUND]
    reduce_sum x5 -> x0, other arithmetic: 54.2 us -> none  [the longest x1 41.1 us: per_device(): elem_hess = hessian.reshape(elements, 4, 24, 24).sum(axis=1)]
    gather x2 -> x0, local copies, waits for them, and re-layouts: 52.6 us -> none  [the longest x1 26.4 us: per_device(): far = flat_scan[source + span_y, layer].astype(jnp.float32)]
    unnamed x16 -> x0, other arithmetic: 51.3 us -> none
    ppermute x14 -> x0, starting transfers between devices: 47.2 us -> none  [from_behind(): return lax.ppermute(block, axis, route)]
  transfers between devices with their start and end apart: 18 -> 4, of which waited for: 13 -> 1; matrix products, arithmetic and copies ran while one was open for 13% -> 6% of each run, Pallas kernels for 0% -> 12%
where the time goes in v1:
time: 148 us; the launch traced here: 147 us
  Pallas kernels  97 us (66%)
  waiting for transfers between devices  17.2 us (12%)
  local copies, waits for them, and re-layouts  13.8 us (9%)
  starting transfers between devices  10.3 us (7%)
  other arithmetic  8.22 us (6%)
    pallas_call x1, Pallas kernels, per_device(): pl.pallas_call(functools.partial(solve_kernel, (n_gx, n_gy), tile_y), out...  55.8 us
    pallas_call x1, Pallas kernels, per_device(): pl.pallas_call(functools.partial(load_kernel, depth, span_y), grid=(tile_...  23.7 us
    pallas_call x1, Pallas kernels, per_device(): pl.pallas_call(functools.partial(hessian_kernel, depth), grid=(tile_x,),...  17.5 us
    ppermute x2, waiting for transfers between devices, extended(): before = lax.ppermute(last, axis, up)  17.2 us
    ppermute x2, starting transfers between devices, extended(): before = lax.ppermute(last, axis, up)  7.72 us
    concatenate x1, other arithmetic, extended(): return jnp.concatenate([before, value, after], axis=dim)  4.52 us
  transfers between devices with their start and end apart: 4, of which 1 were waited for; matrix products, arithmetic and copies ran while one was open for 6% of the time, Pallas kernels for 12%

profile of v1, /device:TPU:0, one launch (start us, length us, event | category | flops | bytes accessed | tf_op | source)
XLA Modules:
  0.0 147.3 jit_solution(12067981482982335925)
XLA Ops:
  0.6 1.1 slice.32
  1.7 5.7 %collective-permute-start = (bf16[4,32,2048]{2,1,0:T(8,128)(2,1)S(1)}, bf16[4,32,2048]{2,1,0:T(8,128)(2,1)}, u32[]{:S(2)}, u32[]{:S(2)}) collective-permute-start(bf16[4,32,2048]{2,1,0:T(8,128)(2,1)S(1)} %slice.32), channel_id=1, source_target_pairs={{0,4},{4,8},{8,12},{12,16},{16,20},{20,24},{24,28},{1,5},{5,9},{9,... | collective-permute-start | bytes 1572872 | tf_op jit(solution)/shard_map/ppermute | solution.py:27
  7.4 2.0 %slice.33 = bf16[5,32,2048]{2,1,0:T(8,128)(2,1)} slice(bf16[16,32,2048]{2,1,0:T(8,128)(2,1)} %param.9), slice={[0:5], [0:32], [0:2048]} | slice | bytes 1310720 | tf_op jit(solution)/shard_map/slice | solution.py:26
  9.4 1.3 collective-permute-start.1
  11.2 0.8 fusion.73
  12.0 0.2 copy.12
  12.2 0.2 squeeze.6
  12.3 0.2 copy.13
  12.5 0.2 squeeze.7
  12.7 0.2 add.1404
  12.9 0.2 add.1408
  13.1 0.7 maximum_maximum_fusion.table_ref
  13.9 0.1 stack.4
  14.0 0.6 add_add_fusion.source_ref
  14.6 17.2 %collective-permute-done = bf16[4,32,2048]{2,1,0:T(8,128)(2,1)} collective-permute-done((bf16[4,32,2048]{2,1,0:T(8,128)(2,1)S(1)}, bf16[4,32,2048]{2,1,0:T(8,128)(2,1)}, u32[]{:S(2)}, u32[]{:S(2)}) %collective-permute-start) | collective-permute-done | bytes 524320 | tf_op jit(solution)/shard_map/ppermute | solution.py:27
  31.8 1.1 constant_dynamic-update-slice_fusion.2
  32.9 1.7 %constant_dynamic-update-slice_fusion.1 = bf16[25,32,2048]{2,1,0:T(8,128)(2,1)S(1)} fusion(bf16[25,32,2048]{2,1,0:T(8,128)(2,1)S(1)} %constant_dynamic-update-slice_fusion.2, bf16[16,32,2048]{2,1,0:T(8,128)(2,1)} %param.9), kind=kLoop, calls=%fused_computation.19 | loop fusion | bytes 4194304
  34.6 1.1 constant_dynamic-update-slice_fusion
  35.8 1.4 fusion.72
  37.1 2.1 %collective-permute-start.2 = (bf16[25,4,2048]{2,1,0:T(4,128)(2,1)}, bf16[25,4,2048]{2,1,0:T(4,128)(2,1)}, u32[]{:S(2)}, u32[]{:S(2)}) collective-permute-start(bf16[25,4,2048]{2,1,0:T(4,128)(2,1)} %get-tuple-element.6), channel_id=1, source_target_pairs={{0,1},{1,2},{2,3},{4,5},{5,6},{6,7},{8,9},{9,10},{10,11},{12,13},{... | collective-permute-start | bytes 1228808 | tf_op jit(solution)/shard_map/ppermute | solution.py:27
  39.2 1.3 collective-permute-start.3
  40.5 0.6 pad_maximum_fusion.3.table_ref
  41.1 17.5 %hessian.1.hess_ref = f32[6,32,16,128]{3,2,1,0:T(8,128)} custom-call(bf16[96,512]{1,0:T(8,128)(2,1)} %pad_maximum_fusion.3.table_ref, bf16[3,16,32,2048]{3,2,1,0:T(8,128)(2,1)} %grad_ref.3, s32[16,32,2048]{2,1,0:T(8,128)} %mask_ref.3), custom_call_target="tpu_custom_call" | custom-call | flops 3221225472 | bytes 10485760 | tf_op jit(solution)/shard_map/hessian/pallas_call | solution.py:422
  58.6 4.5 %pad_maximum_fusion.padded_ref = bf16[25,40,2048]{2,1,0:T(8,128)(2,1)} fusion(bf16[25,4,2048]{2,1,0:T(4,128)(2,1)} %collective-permute-done.3, bf16[25,32,2048]{2,1,0:T(8,128)(2,1)S(1)} %constant_dynamic-update-slice_fusion, bf16[25,4,2048]{2,1,0:T(4,128)(2,1)} %collective-permute-done.2), kind=kLoop, calls=%fused_computation | loop fusion | flops 12288000 | bytes 8192000 | tf_op jit(solution)/shard_map/concatenate | solution.py:29
  63.1 23.7 %load.1.load_ref = f32[3,8,16,128]{3,2,1,0:T(8,128)} custom-call(s32[2048]{0:T(1024)} %add_add_fusion.source_ref, bf16[32,512]{1,0:T(8,128)(2,1)} %maximum_maximum_fusion.table_ref, bf16[25,40,2048]{2,1,0:T(8,128)(2,1)} %pad_maximum_fusion.padded_ref, bf16[16,32,2048]{2,1,0:T(8,128)(2,1)} %scan_ref.1, bf16[16,32,2048]{2,1,0:T(8,128)(2,1)} %weight_ref.1, ...), custom_call_target="tpu_custom_call" | custom-call | tf_op jit(solution)/shard_map/load/pallas_call | solution.py:434
  86.8 55.8 %solve.1 = (f32[6,16,128]{2,1,0:T(8,128)}, f32[6,16,128]{2,1,0:T(8,128)}) custom-call(f32[6,32,16,128]{3,2,1,0:T(8,128)} %hessian.1.hess_ref, f32[3,8,16,128]{3,2,1,0:T(8,128)} %load.1.load_ref), custom_call_target="tpu_custom_call" | custom-call | tf_op jit(solution)/shard_map/solve/pallas_call | solution.py:469
  142.6 0.7 slice.38
  143.3 0.8 slice_bitcast_fusion
  144.1 0.7 slice.36
  144.9 0.8 slice_bitcast_fusion.1
  146.0 0.7 pad_maximum_fusion.2
  146.6 0.7 pad_maximum_fusion.1
  (33 shorter events, 0.8 us)
Async XLA Ops:
  1.7 30.1 %collective-permute-start = (bf16[4,32,2048]{2,1,0:T(8,128)(2,1)S(1)}, bf16[4,32,2048]{2,1,0:T(8,128)(2,1)}, u32[]{:S(2)}, u32[]{:S(2)}) collective-permute-start(bf16[4,32,2048]{2,1,0:T(8,128)(2,1)S(1)} %slice.32), channel_id=1, source_target_pairs={{0,4},{4,8},{8,12},{12,16},{16,20},{20,24},{24,28},{1,5},{5,9},{9,... | collective-permute-start | bytes 1572872 | tf_op jit(solution)/shard_map/ppermute | solution.py:27
  9.4 25.2 %collective-permute-start.1 = (bf16[5,32,2048]{2,1,0:T(8,128)(2,1)}, bf16[5,32,2048]{2,1,0:T(8,128)(2,1)}, u32[]{:S(2)}, u32[]{:S(2)}) collective-permute-start(bf16[5,32,2048]{2,1,0:T(8,128)(2,1)} %slice.33), channel_id=1, source_target_pairs={{4,0},{8,4},{12,8},{16,12},{20,16},{24,20},{28,24},{5,1},{9,5},{13... | collective-permute-start | bytes 1966088 | tf_op jit(solution)/shard_map/ppermute | solution.py:28
  37.1 21.5 %collective-permute-start.2 = (bf16[25,4,2048]{2,1,0:T(4,128)(2,1)}, bf16[25,4,2048]{2,1,0:T(4,128)(2,1)}, u32[]{:S(2)}, u32[]{:S(2)}) collective-permute-start(bf16[25,4,2048]{2,1,0:T(4,128)(2,1)} %get-tuple-element.6), channel_id=1, source_target_pairs={{0,1},{1,2},{2,3},{4,5},{5,6},{6,7},{8,9},{9,10},{10,11},{12,13},{... | collective-permute-start | bytes 1228808 | tf_op jit(solution)/shard_map/ppermute | solution.py:27
  39.2 19.4 %collective-permute-start.3 = (bf16[25,4,2048]{2,1,0:T(4,128)(2,1)}, bf16[25,4,2048]{2,1,0:T(4,128)(2,1)}, u32[]{:S(2)}, u32[]{:S(2)}) collective-permute-start(bf16[25,4,2048]{2,1,0:T(4,128)(2,1)} %get-tuple-element.7), channel_id=1, source_target_pairs={{1,0},{2,1},{3,2},{5,4},{6,5},{7,6},{9,8},{10,9},{11,10},{13,12},{... | collective-permute-start | bytes 1228808 | tf_op jit(solution)/shard_map/ppermute | solution.py:28
